TPU v7x, 32 devices: a whole 2x2x4 slice. The times are simulated.
32 devices in a mesh: parts: 2 (over y), node: 4 (over x, core), local: 4 (over z).
Axes of the slice: x: 2, y: 2, z: 4, core: 2. Of those that a mesh axis runs over, the one named last changes fastest.
Arguments:
- tokens: bfloat16 [4096, 3584], P(('parts', 'node', 'local')), parts along dimension 0, may hold values from -6 to 6
- expert_ids: int32 [4096, 3], P(('parts', 'node', 'local')), parts along dimension 0, may hold values from 0 to 15, all different within a row; in each aligned block of 128 rows (0 to 127, 128 to 255, ...) at most 32 rows name the same one
- gate_weights: float32 [4096, 3], P(('parts', 'node', 'local')), parts along dimension 0, may hold values from 0.1 to 1
- gate_proj: bfloat16 [16, 3584, 1024], P(('node', 'local')), may hold values from -0.09375 to 0.09375
- up_proj: bfloat16 [16, 3584, 1024], P(('node', 'local')), may hold values from -0.09375 to 0.09375
- down_proj: bfloat16 [16, 1024, 3584], P(('node', 'local')), may hold values from -0.1875 to 0.1875
Outputs:
- combined: bfloat16 [4096, 3584], P(('parts', 'node', 'local')), parts along dimension 0
There are 2 independent parts, one for each index of `parts`. A program takes and returns all parts, laid end to end along the dimension named above; an argument that names none is the same for every part. Nothing has to cross between parts.
Inputs may be any that keep to these rules, and one draw needn't show every extreme that they name: `expert_ids`: each row names 3 different experts; among the rows of one device no expert is named by more than 32 rows, a bound that some block reaches.
All inputs are finite; a program needn't handle non-finite values.
Results may differ from a plain program's by a relative error of at most 0.0058.
Values may be sent and summed in bfloat16 or wider, within the bound.
No kernel may reach another device: no remote copies, remote signals or barrier semaphores. Data moves between devices by JAX's collectives and lax.ppermute only.
A program may use at most 128 MiB of HBM per device.

v0:
```python
import jax
import jax.numpy as jnp
from jax import lax
from jax.sharding import PartitionSpec as P

EPG = 4


def expert_rows(received, gate_mat, up_mat, down_mat):
    features = received.shape[-1]
    flattened = received.reshape(-1, features)
    gate_act = jnp.dot(flattened, gate_mat, preferred_element_type=jnp.float32)
    up_act = jnp.dot(flattened, up_mat, preferred_element_type=jnp.float32)
    hidden = (jax.nn.silu(gate_act) * up_act).astype(jnp.bfloat16)
    output = jnp.dot(hidden, down_mat, preferred_element_type=jnp.float32).astype(jnp.bfloat16)
    return output.reshape(received.shape)


def on_device(tokens, expert_ids, gate_weights, gate_proj, up_proj, down_proj):
    tok_dev = tokens.shape[0]
    features = tokens.shape[1]
    top_count = expert_ids.shape[1]
    node_count = lax.axis_size("node")
    local_count = lax.axis_size("local")
    experts = EPG * node_count
    wsplit = local_count // EPG
    capacity = 4 * tok_dev * top_count // (3 * experts)
    matches = expert_ids[:, :, None] == jnp.arange(experts, dtype=jnp.int32)[None, None, :]
    chosen = jnp.sum(matches.astype(jnp.int32), axis=1)
    ranking = jnp.cumsum(chosen, axis=0) - chosen
    slot_ids = jnp.arange(capacity, dtype=jnp.int32)
    selected = (chosen.T[:, None, :] == 1) & (ranking.T[:, None, :] == slot_ids[None, :, None])
    selected_flat = selected.reshape(experts * capacity, tok_dev)
    packed_rows = jnp.dot(
        selected_flat.astype(jnp.bfloat16), tokens, preferred_element_type=jnp.float32
    ).astype(jnp.bfloat16)
    gate_mat = gate_proj[0]
    up_mat = up_proj[0]
    down_mat = down_proj[0]
    packed = jnp.broadcast_to(
        packed_rows.reshape(experts, 1, capacity, features), (experts, wsplit, capacity, features)
    )
    outgoing = packed.reshape(node_count * local_count, capacity, features)
    outputs = expert_rows(
        lax.all_to_all(outgoing, ("node", "local"), split_axis=0, concat_axis=0, tiled=True),
        gate_mat,
        up_mat,
        down_mat,
    )
    returned = lax.all_to_all(outputs, ("node", "local"), split_axis=0, concat_axis=0, tiled=True)
    summed = jnp.sum(
        returned.reshape(experts, wsplit, capacity, features).astype(jnp.float32), axis=1
    )
    summed = summed.reshape(experts * capacity, features)
    slot_rank = jnp.take_along_axis(ranking, expert_ids, axis=1)
    row_index = expert_ids * capacity + slot_rank
    picked = summed[row_index]
    combined = jnp.sum(picked * gate_weights[:, :, None], axis=1)
    return combined.astype(jnp.bfloat16)


def solution(mesh):
    return jax.shard_map(
        on_device,
        mesh=mesh,
        in_specs=(
            P(("parts", "node", "local"), None),
            P(("parts", "node", "local"), None),
            P(("parts", "node", "local"), None),
            P(("node", "local"), None, None),
            P(("node", "local"), None, None),
            P(("node", "local"), None, None),
        ),
        out_specs=P(("parts", "node", "local"), None),
        check_vma=False,
    )
```

profile of v0, /device:TPU:0, one launch (start us, length us, event | category | flops | bytes accessed | tf_op | source)
XLA Modules:
  0.0 236.9 jit_solution(13579295022008865182)
XLA Ops:
  0.0 0.0 copy-start
  0.0 0.8 convert_reduce_fusion
  0.8 0.1 copy.33
  0.9 0.2 reduce_window_sum.11
  1.1 0.1 copy.35
  1.1 0.1 eq.52
  1.2 0.2 fusion.13
  1.4 0.0 copy-done
  1.4 0.0 copy-start.4
  1.4 1.1 convolution_convert_fusion
  2.5 90.5 %all_to_all.10 = bf16[16,32,3584]{2,1,0:T(8,128)(2,1)S(1)} all-to-all(bf16[16,32,3584]{2,1,0:T(8,128)(2,1)S(1)} %bitcast.39), channel_id=1, replica_groups=mesh['parts'=2,'node'=4,'local'=4] {'node','local'}, dimensions={0} | all-to-all | bytes 7340032 | tf_op jit(solution)/shard_map/all_to_all | solution.py:45
  93.0 1.8 copy-done.1
  94.8 0.0 copy-done.4
  94.8 3.9 %fusion.2 = f32[512,1024]{1,0:T(8,128)S(1)} fusion(bf16[512,3584]{1,0:T(8,128)(2,1)S(1)} %bitcast.41, bf16[1,3584,1024]{2,1,0:T(8,128)(2,1)S(1)} %copy-done.4), kind=kOutput, calls=%fused_computation.4 | convolution fusion | flops 3758096384 | bytes 13107200 | tf_op jit(solution)/shard_map/dot_general | solution.py:13
  98.8 16.0 %fusion.6 = bf16[512,3584]{1,0:T(8,128)(2,1)} fusion(bf16[1,1024,3584]{2,1,0:T(8,128)(2,1)} %param.11, f32[512,1024]{1,0:T(8,128)S(1)} %fusion.2, bf16[512,3584]{1,0:T(8,128)(2,1)} %bitcast.42, bf16[1,3584,1024]{2,1,0:T(8,128)(2,1)} %param.9), kind=kOutput, calls=%fused_computation.9 | convolution fusion | flops 7521173504 | bytes 24117248 | tf_op jit(solution)/shard_map/dot_general | solution.py:15
  114.8 4.8 %all-to-all-start.1 = ((bf16[16,32,3584]{2,1,0:T(8,128)(2,1)}), bf16[16,32,3584]{2,1,0:T(8,128)(2,1)}, u32[]{:S(2)}, u32[]{:S(2)}) async-start(bf16[16,32,3584]{2,1,0:T(8,128)(2,1)} %bitcast.40), calls=%async_computation.1 | async-start | bytes 7340032 | tf_op jit(solution)/shard_map/all_to_all | solution.py:50
  119.6 0.0 copy-done.2
  119.6 0.1 copy.36
  119.7 0.2 reshape.50
  119.9 0.0 copy-start.3
  119.9 2.9 %gather_fusion.1 = s32[384]{0:T(512)S(1)} fusion(s32[128,16]{1,0:T(8,128)S(1)} %sub.7, s32[384]{0:T(512)S(1)} %reshape.50), kind=kCustom, calls=%fused_computation.1 | custom fusion | bytes 6144 | tf_op jit(solution)/shard_map/jit(take_along_axis)/gather | solution.py:55
  122.8 0.2 reshape.53
  123.0 0.1 copy.37
  123.1 0.1 copy.38
  123.2 0.2 reshape.44
  123.5 0.0 copy-done.3
  123.5 0.1 copy.39
  123.6 78.9 %all-to-all-done.1 = bf16[16,32,3584]{2,1,0:T(8,128)(2,1)} async-done(((bf16[16,32,3584]{2,1,0:T(8,128)(2,1)}), bf16[16,32,3584]{2,1,0:T(8,128)(2,1)}, u32[]{:S(2)}, u32[]{:S(2)}) %all-to-all-start.1) | async-done | bytes 3670048 | tf_op jit(solution)/shard_map/all_to_all | solution.py:50
  202.5 6.0 %bitcast_convert_fusion = f32[512,3584]{1,0:T(8,128)} fusion(bf16[16,32,3584]{2,1,0:T(8,128)(2,1)} %all-to-all-done.1), kind=kLoop, calls=%fused_computation.11 | loop fusion | flops 1835008 | bytes 11010048 | tf_op jit(solution)/shard_map/reshape | solution.py:54
  208.4 10.7 %gather_fusion = f32[384,3584]{1,0:T(8,128)} fusion(f32[512,3584]{1,0:T(8,128)} %bitcast_convert_fusion, s32[1024]{0:T(1024)S(1)} %pad_clamp_fusion), kind=kCustom, calls=%fused_computation | custom fusion | bytes 11011584 | tf_op jit(solution)/shard_map/gather | solution.py:57
  219.1 8.5 %reshape.43 = f32[128,3,3584]{2,1,0:T(4,128)} reshape(f32[384,3584]{1,0:T(8,128)} %gather_fusion) | data formatting | bytes 11010048 | tf_op jit(solution)/shard_map/gather | solution.py:57
  227.6 9.3 %multiply_reduce_fusion = bf16[128,3584]{1,0:T(8,128)(2,1)} fusion(f32[128,3,3584]{2,1,0:T(4,128)} %reshape.43, f32[128,3]{1,0:T(8,128)S(1)} %copy.39), kind=kLoop, calls=%fused_computation.8 | loop fusion | flops 2293760 | bytes 6424064 | tf_op jit(solution)/shard_map/reduce_sum | solution.py:58
  (8 shorter events, 0.0 us)
Async XLA Ops:
  0.0 1.4 copy-start
  1.4 93.5 %copy-start.4 = (bf16[1,3584,1024]{2,1,0:T(8,128)(2,1)S(1)}, bf16[1,3584,1024]{2,1,0:T(8,128)(2,1)}, u32[]{:S(2)}) copy-start(bf16[1,3584,1024]{2,1,0:T(8,128)(2,1)} %param.10) | copy-start | bytes 22020100
  93.0 1.8 copy-start.1
  114.7 4.8 %copy-start.2 = (s32[128,3]{0,1:T(4,128)S(1)}, s32[128,3]{0,1:T(4,128)}, u32[]{:S(2)}) copy-start(s32[128,3]{0,1:T(4,128)} %param.7) | copy-start | bytes 4612
  114.8 87.7 %all-to-all-start.1 = ((bf16[16,32,3584]{2,1,0:T(8,128)(2,1)}), bf16[16,32,3584]{2,1,0:T(8,128)(2,1)}, u32[]{:S(2)}, u32[]{:S(2)}) async-start(bf16[16,32,3584]{2,1,0:T(8,128)(2,1)} %bitcast.40), calls=%async_computation.1 | async-start | bytes 7340032 | tf_op jit(solution)/shard_map/all_to_all | solution.py:50
  119.9 3.5 %copy-start.3 = (f32[128,3]{0,1:T(4,128)S(1)}, f32[128,3]{0,1:T(4,128)}, u32[]{:S(2)}) copy-start(f32[128,3]{0,1:T(4,128)} %param.8) | copy-start | bytes 4612
where the time goes:
time: 237 us
  blocking collectives  90.5 us (38%)
  waiting for transfers between devices  78.9 us (33%)
  local copies, waits for them, and re-layouts  25.2 us (11%)
  matrix products  21 us (9%)
  other arithmetic  16.4 us (7%)
  starting transfers between devices  4.82 us (2%)
    all_to_all x1, blocking collectives, on_device(): lax.all_to_all(outgoing, ('node', 'local'), split_axis=0, concat_axis=0,...  90.5 us
    all_to_all x1, waiting for transfers between devices, on_device(): lax.all_to_all(outputs, ('node', 'local'), split_axis=0, concat_axis=0, t...  78.9 us
    gather x2, local copies, waits for them, and re-layouts, on_device(): picked = summed[row_index]  19.2 us
    dot_general x1, matrix products, expert_rows(): jnp.dot(hidden, down_mat, preferred_element_type=jnp.float32)  16 us
    reduce_sum x1, other arithmetic, on_device(): combined = jnp.sum(picked * gate_weights[:, :, None], axis=1)  9.26 us
    reshape x1, other arithmetic, on_device(): summed = summed.reshape(experts * capacity, features)  5.96 us
    all_to_all x1, starting transfers between devices, on_device(): lax.all_to_all(outputs, ('node', 'local'), split_axis=0, concat_axis=0, t...  4.82 us
  transfers between devices with their start and end apart: 1, of which 1 were waited for; matrix products, arithmetic and copies ran while one was open for 2% of the time, Pallas kernels for 0%

commit v1 on v0

v1 whole, which is shorter than its diff:
```python
import jax
import jax.numpy as jnp
from jax import lax
from jax.sharding import PartitionSpec as P

EPG = 4
IN_CHUNKS = 1
OUT_CHUNKS = 1


def on_device(tokens, expert_ids, gate_weights, gate_proj, up_proj, down_proj):
    tok_dev, features = tokens.shape
    top_count = expert_ids.shape[1]
    node_count = lax.axis_size("node")
    local_count = lax.axis_size("local")
    experts = EPG * node_count
    wsplit = local_count // EPG
    capacity = 4 * tok_dev * top_count // (3 * experts)
    devices = node_count * local_count
    slots = devices * capacity
    axes = ("node", "local")

    matches = expert_ids[:, :, None] == jnp.arange(experts, dtype=jnp.int32)[None, None, :]
    chosen = jnp.sum(matches.astype(jnp.int32), axis=1)
    weight = jnp.sum(jnp.where(matches, gate_weights[:, :, None], 0.0), axis=1)
    ranking = jnp.cumsum(chosen, axis=0) - chosen
    slot_ids = jnp.arange(capacity, dtype=jnp.int32)
    selected = (chosen.T[:, None, :] == 1) & (ranking.T[:, None, :] == slot_ids[None, :, None])
    pick = jnp.broadcast_to(selected[:, None], (experts, wsplit, capacity, tok_dev))
    pick = pick.reshape(slots, tok_dev)
    scale = jnp.broadcast_to(
        jnp.where(selected, weight.T[:, None, :], 0.0)[:, None], (experts, wsplit, capacity, tok_dev)
    ).reshape(slots, tok_dev)
    scale_high = scale.astype(jnp.bfloat16)
    scale_low = (scale - scale_high.astype(jnp.float32)).astype(jnp.bfloat16)

    gate_mat, up_mat, down_mat = gate_proj[0], up_proj[0], down_proj[0]
    pick = pick.astype(jnp.bfloat16)

    step = features // IN_CHUNKS
    gate_act = up_act = None
    for part in range(IN_CHUNKS):
        cols = slice(part * step, (part + 1) * step)
        packed = jnp.dot(pick, tokens[:, cols], preferred_element_type=jnp.float32).astype(jnp.bfloat16)
        rows = lax.all_to_all(
            packed.reshape(devices, capacity, step), axes, split_axis=0, concat_axis=0, tiled=True
        ).reshape(slots, step)
        gate_part = jnp.dot(rows, gate_mat[cols], preferred_element_type=jnp.float32)
        up_part = jnp.dot(rows, up_mat[cols], preferred_element_type=jnp.float32)
        gate_act = gate_part if part == 0 else gate_act + gate_part
        up_act = up_part if part == 0 else up_act + up_part
    hidden = (jax.nn.silu(gate_act) * up_act).astype(jnp.bfloat16)

    step = features // OUT_CHUNKS
    pieces = []
    for part in range(OUT_CHUNKS):
        cols = slice(part * step, (part + 1) * step)
        output = jnp.dot(hidden, down_mat[:, cols], preferred_element_type=jnp.float32).astype(jnp.bfloat16)
        returned = lax.all_to_all(
            output.reshape(devices, capacity, step), axes, split_axis=0, concat_axis=0, tiled=True
        ).reshape(slots, step)
        contract = (((0,), (0,)), ((), ()))
        total = lax.dot_general(scale_high, returned, contract, preferred_element_type=jnp.float32)
        total += lax.dot_general(scale_low, returned, contract, preferred_element_type=jnp.float32)
        pieces.append(total.astype(jnp.bfloat16))
    return pieces[0] if OUT_CHUNKS == 1 else jnp.concatenate(pieces, axis=1)


def solution(mesh):
    row = P(("parts", "node", "local"), None)
    mat = P(("node", "local"), None, None)
    return jax.shard_map(
        on_device,
        mesh=mesh,
        in_specs=(row, row, row, mat, mat, mat),
        out_specs=row,
        check_vma=False,
    )
```

time: 237 us -> 209 us (0.88)
  local copies, waits for them, and re-layouts: 25.2 us -> 2.09 us
  other arithmetic: 16.4 us -> 1.13 us
  matrix products: 21 us -> 27.4 us
  waiting for transfers between devices: 78.9 us -> 83 us
    gather x7 -> x0, local copies, waits for them, and re-layouts: 22.6 us -> none  [the longest x2 19.2 us: on_device(): picked = summed[row_index]]
    reduce_sum x1, other arithmetic: 9.26 us -> 0.01 us  [on_device(): weight = jnp.sum(jnp.where(matches, gate_weights[:, :, None], 0.0), axis=1)]
    dot_general x3 -> x5, matrix products: 21 us -> 27.4 us  [the longest x1 16 us: on_device(): jnp.dot(hidden, down_mat[:, cols], preferred_element_type=jnp.float32)]
    reshape x1 -> x0, other arithmetic: 5.96 us -> none  [on_device(): summed = summed.reshape(experts * capacity, features)]
    all_to_all x1, waiting for transfers between devices: 78.9 us -> 83 us  [on_device(): lax.all_to_all(output.reshape(devices, capacity, step), axes, split_axis=...]
  transfers between devices with their start and end apart: 1 -> 1, of which waited for: 1 -> 1; matrix products, arithmetic and copies ran while one was open for 2% -> 0% of each run, Pallas kernels for 0% -> 0%
where the time goes in v1:
time: 209 us
  blocking collectives  90.5 us (43%)
  waiting for transfers between devices  83 us (40%)
  matrix products  27.4 us (13%)
  starting transfers between devices  4.64 us (2%)
  local copies, waits for them, and re-layouts  2.09 us (1%)
    all_to_all x1, blocking collectives, on_device(): lax.all_to_all(packed.reshape(devices, capacity, step), axes, split_axis=...  90.5 us
    all_to_all x1, waiting for transfers between devices, on_device(): lax.all_to_all(output.reshape(devices, capacity, step), axes, split_axis=...  83 us
    dot_general x1, matrix products, on_device(): jnp.dot(hidden, down_mat[:, cols], preferred_element_type=jnp.float32)  16 us
    all_to_all x1, starting transfers between devices, on_device(): lax.all_to_all(output.reshape(devices, capacity, step), axes, split_axis=...  4.64 us
  transfers between devices with their start and end apart: 1, of which 1 were waited for; matrix products, arithmetic and copies ran while one was open for 0% of the time, Pallas kernels for 0%

profile of v1, /device:TPU:0, one launch (start us, length us, event | category | flops | bytes accessed | tf_op | source)
XLA Modules:
  0.0 208.9 jit_solution(2327508818410015779)
XLA Ops:
  0.0 0.0 copy-start
  0.0 0.8 convert_reduce_fusion
  0.8 0.1 copy.11
  0.9 0.2 reduce_window_sum.11
  1.1 0.1 copy.13
  1.1 0.1 eq.61
  1.2 0.2 fusion.17
  1.4 0.0 copy-done
  1.4 1.1 convolution_convert_fusion
  2.5 0.0 copy-start.4
  2.5 90.5 %all_to_all.10 = bf16[16,32,3584]{2,1,0:T(8,128)(2,1)S(1)} all-to-all(bf16[16,32,3584]{2,1,0:T(8,128)(2,1)S(1)} %bitcast.43), channel_id=1, replica_groups=mesh['parts'=2,'node'=4,'local'=4] {'node','local'}, dimensions={0} | all-to-all | bytes 7340032 | tf_op jit(solution)/shard_map/all_to_all | solution.py:45
  93.0 0.0 copy-start.1
  93.0 1.8 copy-done.1
  94.8 0.0 copy-done.4
  94.8 3.9 %fusion.2 = f32[512,1024]{1,0:T(8,128)S(1)} fusion(bf16[512,3584]{1,0:T(8,128)(2,1)S(1)} %bitcast.45, bf16[1,3584,1024]{2,1,0:T(8,128)(2,1)S(1)} %copy-done.4), kind=kOutput, calls=%fused_computation.2 | convolution fusion | flops 3758096384 | bytes 13107200 | tf_op jit(solution)/shard_map/dot_general | solution.py:49
  98.8 16.0 %fusion.6 = bf16[512,3584]{1,0:T(8,128)(2,1)} fusion(bf16[1,1024,3584]{2,1,0:T(8,128)(2,1)} %param.11, f32[512,1024]{1,0:T(8,128)S(1)} %fusion.2, bf16[512,3584]{1,0:T(8,128)(2,1)} %bitcast.46, bf16[1,3584,1024]{2,1,0:T(8,128)(2,1)} %param.9), kind=kOutput, calls=%fused_computation.6 | convolution fusion | flops 7521173504 | bytes 24117248 | tf_op jit(solution)/shard_map/dot_general | solution.py:58
  114.8 0.0 copy-start.2
  114.8 0.0 copy-start.3
  114.8 4.6 %all-to-all-start.1 = ((bf16[16,32,3584]{2,1,0:T(8,128)(2,1)}), bf16[16,32,3584]{2,1,0:T(8,128)(2,1)}, u32[]{:S(2)}, u32[]{:S(2)}) async-start(bf16[16,32,3584]{2,1,0:T(8,128)(2,1)} %bitcast.44), calls=%async_computation.1 | async-start | bytes 7340032 | tf_op jit(solution)/shard_map/all_to_all | solution.py:59
  119.4 0.0 copy-done.2
  119.4 0.0 copy-done.3
  119.5 83.0 %all-to-all-done.1 = bf16[16,32,3584]{2,1,0:T(8,128)(2,1)} async-done(((bf16[16,32,3584]{2,1,0:T(8,128)(2,1)}), bf16[16,32,3584]{2,1,0:T(8,128)(2,1)}, u32[]{:S(2)}, u32[]{:S(2)}) %all-to-all-start.1) | async-done | bytes 3670048 | tf_op jit(solution)/shard_map/all_to_all | solution.py:59
  202.5 2.7 %convolution_bitcast_fusion = f32[128,3584]{1,0:T(8,128)S(1)} fusion(bf16[16,32,3584]{2,1,0:T(8,128)(2,1)} %all-to-all-done.1, f32[16,128]{1,0:T(8,128)S(1)} %bitcast.47, s32[16,128]{1,0:T(8,128)S(1)} %copy.13, pred[16,128]{1,0:T(8,128)(4,1)S(1)} %compare_bitcast_fusion), kind=kOutput, calls=%fused_computation.8 | convolution fusion | flops 470220800 | bytes 5523456 | tf_op jit(solution)/shard_map/dot_general | solution.py:64
  205.2 3.7 %fusion.10 = bf16[128,3584]{1,0:T(8,128)(2,1)} fusion(f32[128,3584]{1,0:T(8,128)S(1)} %convolution_bitcast_fusion, bf16[16,32,3584]{2,1,0:T(8,128)(2,1)} %all-to-all-done.1, f32[16,128]{1,0:T(8,128)S(1)} %bitcast.48, s32[16,128]{1,0:T(8,128)S(1)} %copy.13, pred[16,128]{1,0:T(8,128)(4,1)S(1)} %compare_bitcast_fusion), kind=kOutput, calls=%fused_computation.11 | convolution fusion | flops 470876160 | bytes 6440960 | tf_op jit(solution)/shard_map/dot_general | solution.py:63
  (4 shorter events, 0.0 us)
Async XLA Ops:
  0.0 1.4 copy-start
  2.5 92.4 %copy-start.4 = (bf16[1,3584,1024]{2,1,0:T(8,128)(2,1)S(1)}, bf16[1,3584,1024]{2,1,0:T(8,128)(2,1)}, u32[]{:S(2)}) copy-start(bf16[1,3584,1024]{2,1,0:T(8,128)(2,1)} %param.10) | copy-start | bytes 22020100
  93.0 1.8 copy-start.1
  114.8 4.7 %copy-start.2 = (s32[128,3]{0,1:T(4,128)S(1)}, s32[128,3]{0,1:T(4,128)}, u32[]{:S(2)}) copy-start(s32[128,3]{0,1:T(4,128)} %param.7) | copy-start | bytes 4612
  114.8 4.7 %copy-start.3 = (f32[128,3]{0,1:T(4,128)S(1)}, f32[128,3]{0,1:T(4,128)}, u32[]{:S(2)}) copy-start(f32[128,3]{0,1:T(4,128)} %param.8) | copy-start | bytes 4612
  114.8 87.7 %all-to-all-start.1 = ((bf16[16,32,3584]{2,1,0:T(8,128)(2,1)}), bf16[16,32,3584]{2,1,0:T(8,128)(2,1)}, u32[]{:S(2)}, u32[]{:S(2)}) async-start(bf16[16,32,3584]{2,1,0:T(8,128)(2,1)} %bitcast.44), calls=%async_computation.1 | async-start | bytes 7340032 | tf_op jit(solution)/shard_map/all_to_all | solution.py:59

commit v2 on v1

v2 whole, which is shorter than its diff:
```python
import jax
import jax.numpy as jnp
from jax import lax
from jax.experimental import pallas as pl
from jax.experimental.pallas import tpu as pltpu
from jax.sharding import PartitionSpec as P


EPG = 4
AXES = ("node", "local")


def dot(a, b):
    return jnp.dot(a, b, preferred_element_type=jnp.float32)


def routing(expert_ids, gate_weights, shards, wsplit, capacity):
    matches = expert_ids[None] == (shards // wsplit)[:, None, None]
    chosen = jnp.sum(matches.astype(jnp.int32), axis=1)
    weight = jnp.sum(jnp.where(matches, gate_weights[None], 0.0), axis=1)
    ranking = jnp.cumsum(chosen, axis=1) - chosen
    slot_ids = jnp.arange(capacity, dtype=jnp.int32)
    selected = (chosen[:, None, :] == 1) & (ranking[:, None, :] == slot_ids[None, :, None])
    scale = jnp.where(selected, weight[:, None, :], 0.0)
    slots = shards.shape[0] * capacity
    high = lax.reduce_precision(scale, exponent_bits=8, mantissa_bits=7)
    low = (scale - high).astype(jnp.bfloat16)
    flat = lambda a: a.reshape(slots, -1)
    return flat(selected.astype(jnp.bfloat16)), flat(high.astype(jnp.bfloat16)), flat(low)


def weighted_rows(high, low, rows):
    contract = (((0,), (0,)), ((), ()))
    total = lax.dot_general(high, rows, contract, preferred_element_type=jnp.float32)
    return total + lax.dot_general(low, rows, contract, preferred_element_type=jnp.float32)


VMEM_WHOLE = pl.BlockSpec(memory_space=pltpu.VMEM)
HBM_WHOLE = pl.BlockSpec(memory_space=pl.ANY)
UP_GROUPS, DOWN_GROUPS, LANES = 4, 2, 512


def groups_of(size, count):
    tiles = size // 128
    count = min(count, tiles)
    edges = [tiles * i // count * 128 for i in range(count + 1)]
    return [pl.ds(a, b - a) for a, b in zip(edges, edges[1:])]


def ffn_kernel(rows_ref, gate_hbm, up_hbm, down_hbm, out_ref, *scratch):
    gate_buf, up_buf, down_buf, gate_sum, up_sum, hidden_ref, gate_sem, up_sem, down_sem = scratch
    depth, width = gate_buf.shape
    up_groups, down_groups = groups_of(depth, UP_GROUPS), groups_of(depth, DOWN_GROUPS)
    gates = [pltpu.make_async_copy(gate_hbm.at[g], gate_buf.at[g], gate_sem.at[i]) for i, g in enumerate(up_groups)]
    ups = [pltpu.make_async_copy(up_hbm.at[g], up_buf.at[g], up_sem.at[i]) for i, g in enumerate(up_groups)]
    downs = [
        pltpu.make_async_copy(down_hbm.at[:, g], down_buf.at[:, g], down_sem.at[i])
        for i, g in enumerate(down_groups)
    ]
    for gate, up in zip(gates, ups):
        gate.start()
        up.start()
    for down in downs:
        down.start()
    tiles = [pl.ds(at, min(LANES, width)) for at in range(0, width, LANES)]
    for i, (group, gate, up) in enumerate(zip(up_groups, gates, ups)):
        for copy, buf, total in ((gate, gate_buf, gate_sum), (up, up_buf, up_sum)):
            copy.wait()
            for tile in tiles:
                value = dot(rows_ref[:, group], buf[group, tile])
                total[:, tile] = value if i == 0 else total[:, tile] + value
    for tile in tiles:
        hidden_ref[:, tile] = (jax.nn.silu(gate_sum[:, tile]) * up_sum[:, tile]).astype(jnp.bfloat16)
    for group, down in zip(down_groups, downs):
        down.wait()
        out_ref[:, group] = dot(hidden_ref[...], down_buf[:, group]).astype(jnp.bfloat16)


def ffn(rows, gate_mat, up_mat, down_mat):
    count, features = rows.shape
    width = gate_mat.shape[1]
    return pl.pallas_call(
        ffn_kernel,
        in_specs=[VMEM_WHOLE] + [HBM_WHOLE] * 3,
        out_specs=VMEM_WHOLE,
        out_shape=jax.ShapeDtypeStruct((count, features), jnp.bfloat16),
        scratch_shapes=[pltpu.VMEM(mat.shape, jnp.bfloat16) for mat in (gate_mat, up_mat, down_mat)]
        + [pltpu.VMEM((count, width), kind) for kind in (jnp.float32, jnp.float32, jnp.bfloat16)]
        + [pltpu.SemaphoreType.DMA((n,)) for n in (UP_GROUPS, UP_GROUPS, DOWN_GROUPS)],
        compiler_params=pltpu.CompilerParams(vmem_limit_bytes=48 << 20),
        cost_estimate=pl.CostEstimate(
            flops=6 * count * width * features,
            bytes_accessed=6 * width * features + 4 * count * features,
            transcendentals=count * width,
        ),
    )(rows, gate_mat, up_mat, down_mat)


def on_device(tokens, expert_ids, gate_weights, gate_proj, up_proj, down_proj):
    tok_dev, _ = tokens.shape
    top_count = expert_ids.shape[1]
    node_count = lax.axis_size("node")
    local_count = lax.axis_size("local")
    capacity = 4 * tok_dev * top_count // (3 * EPG * node_count)
    wsplit = local_count // EPG
    half = local_count // 2
    groups = [
        [n * local_count + side * half + i for n in range(node_count) for i in range(half)]
        for side in range(2)
    ]
    members = node_count * half
    slots = members * capacity
    gate_mat, up_mat, down_mat = gate_proj[0], up_proj[0], down_proj[0]

    across = [(i, (i + half) % local_count) for i in range(local_count)]

    def cross(array):
        return lax.ppermute(array, "local", across)

    def swap(rows):
        width = rows.shape[1]
        moved = lax.all_to_all(rows.reshape(members, capacity, width), AXES, 0, 0, axis_index_groups=groups, tiled=True)
        return moved.reshape(slots, width)

    ids, weights = expert_ids.T, gate_weights.T
    table = cross(jnp.concatenate([ids.astype(jnp.float32), weights]))
    far_tokens = cross(tokens)
    member = jnp.arange(members, dtype=jnp.int32)
    first = lax.axis_index("local") // half * half
    shards = member // half * local_count + first + member % half

    pick, high, low = routing(ids, weights, shards, wsplit, capacity)
    rows = swap(dot(pick, tokens).astype(jnp.bfloat16))
    rows, table, far_tokens = lax.optimization_barrier((rows, table, far_tokens))
    far_pick, far_high, far_low = routing(
        table[:top_count].astype(jnp.int32), table[top_count:], shards, wsplit, capacity
    )
    far_tokens, far_pick, far_high, far_low, high, low = lax.optimization_barrier(
        (far_tokens, far_pick, far_high, far_low, high, low)
    )
    far_rows = swap(dot(far_pick, far_tokens).astype(jnp.bfloat16))
    output = ffn(rows, gate_mat, up_mat, down_mat)
    far_output = ffn(far_rows, gate_mat, up_mat, down_mat)
    far_returned = swap(far_output)
    arrived = cross(weighted_rows(far_high, far_low, far_returned).astype(jnp.bfloat16))
    returned = swap(output)
    return (weighted_rows(high, low, returned) + arrived.astype(jnp.float32)).astype(jnp.bfloat16)


def solution(mesh):
    row = P(("parts", "node", "local"), None)
    mat = P(("node", "local"), None, None)

    return jax.shard_map(
        on_device,
        mesh=mesh,
        in_specs=(row, row, row, mat, mat, mat),
        out_specs=row,
        check_vma=False,
    )
```

time: 209 us -> 174 us (0.83)
  blocking collectives: 90.5 us -> 27.5 us
  Pallas kernels: 0 us -> 19.5 us
  matrix products: 27.4 us -> 10.6 us
  starting transfers between devices: 4.64 us -> 19.1 us
  waiting for transfers between devices: 83 us -> 92.5 us
    all_to_all x1, blocking collectives: 90.5 us -> 27.5 us  [swap(): lax.all_to_all(rows.reshape(members, capacity, width), AXES, 0, 0, axis_i...]
    ppermute x0 -> x3, waiting for transfers between devices: none -> 44.6 us  [cross(): return lax.ppermute(array, 'local', across)]
    all_to_all x1 -> x3, waiting for transfers between devices: 83 us -> 47.9 us  [swap(): lax.all_to_all(rows.reshape(members, capacity, width), AXES, 0, 0, axis_i...]
    pallas_call x0 -> x2, Pallas kernels: none -> 19.5 us  [ffn(): pl.pallas_call(ffn_kernel, in_specs=[VMEM_WHOLE] + [HBM_WHOLE] * 3, out_s...]
    dot_general x5 -> x6, matrix products: 27.4 us -> 10.6 us  [the longest x2 4.6 us: weighted_rows(): lax.dot_general(low, rows, contract, preferred_element_type=jnp.float32)]
    all_to_all x1 -> x3, starting transfers between devices: 4.64 us -> 13.3 us  [swap(): lax.all_to_all(rows.reshape(members, capacity, width), AXES, 0, 0, axis_i...]
    ppermute x0 -> x3, starting transfers between devices: none -> 5.79 us  [cross(): return lax.ppermute(array, 'local', across)]
  transfers between devices with their start and end apart: 1 -> 6, of which waited for: 1 -> 5; matrix products, arithmetic and copies ran while one was open for 0% -> 2% of each run, Pallas kernels for 0% -> 6%
where the time goes in v2:
time: 174 us
  waiting for transfers between devices  92.5 us (53%)
  blocking collectives  27.5 us (16%)
  Pallas kernels  19.5 us (11%)
  starting transfers between devices  19.1 us (11%)
  matrix products  10.6 us (6%)
  local copies, waits for them, and re-layouts  2.58 us (1%)
  other arithmetic  1.86 us (1%)
    all_to_all x3, waiting for transfers between devices, swap(): lax.all_to_all(rows.reshape(members, capacity, width), AXES, 0, 0, axis_i...  47.9 us
    ppermute x3, waiting for transfers between devices, cross(): return lax.ppermute(array, 'local', across)  44.6 us
    all_to_all x1, blocking collectives, swap(): lax.all_to_all(rows.reshape(members, capacity, width), AXES, 0, 0, axis_i...  27.5 us
    pallas_call x2, Pallas kernels, ffn(): pl.pallas_call(ffn_kernel, in_specs=[VMEM_WHOLE] + [HBM_WHOLE] * 3, out_s...  19.5 us
    all_to_all x3, starting transfers between devices, swap(): lax.all_to_all(rows.reshape(members, capacity, width), AXES, 0, 0, axis_i...  13.3 us
    ppermute x3, starting transfers between devices, cross(): return lax.ppermute(array, 'local', across)  5.79 us
    dot_general x2, matrix products, weighted_rows(): lax.dot_general(low, rows, contract, preferred_element_type=jnp.float32)  4.6 us
    dot_general x2, matrix products, dot(): return jnp.dot(a, b, preferred_element_type=jnp.float32)  3.68 us
  transfers between devices with their start and end apart: 6, of which 5 were waited for; matrix products, arithmetic and copies ran while one was open for 2% of the time, Pallas kernels for 6%

profile of v2, /device:TPU:0, one launch (start us, length us, event | category | flops | bytes accessed | tf_op | source)
XLA Modules:
  0.0 173.7 jit_solution(13713041996934953590)
XLA Ops:
  0.0 0.8 fusion.6
  0.8 0.3 reduce_window_sum.17
  1.1 0.1 eq.93
  1.1 0.1 fusion.3
  1.3 3.1 %convolution_convert_fusion.1 = bf16[256,3584]{1,0:T(8,128)(2,1)} fusion(pred[256,128]{1,0:T(32,128)(4,1)S(1)} %fusion.3, bf16[128,3584]{1,0:T(8,128)(2,1)} %param.6), kind=kOutput, calls=%fused_computation.1 | convolution fusion | flops 235798528 | bytes 2785280 | tf_op jit(solution)/shard_map/dot_general | solution.py:14
  4.3 5.4 %all-to-all-start = ((bf16[8,32,3584]{2,1,0:T(8,128)(2,1)}), bf16[8,32,3584]{2,1,0:T(8,128)(2,1)S(1)}, u32[]{:S(2)}, u32[]{:S(2)}) async-start(bf16[8,32,3584]{2,1,0:T(8,128)(2,1)} %bitcast.82), calls=%async_computation | async-start | bytes 3670016 | tf_op jit(solution)/shard_map/all_to_all | solution.py:122
  9.7 2.6 %collective-permute-start.1 = (bf16[128,3584]{1,0:T(8,128)(2,1)}, bf16[128,3584]{1,0:T(8,128)(2,1)S(1)}, u32[]{:S(2)}, u32[]{:S(2)}) collective-permute-start(bf16[128,3584]{1,0:T(8,128)(2,1)} %param.6), channel_id=1, source_target_pairs={{0,2},{1,3},{2,0},{3,1},{4,6},{5,7},{6,4},{7,5},{8,10},{9,11},{10,... | collective-permute-start | bytes 2752520 | tf_op jit(solution)/shard_map/ppermute | solution.py:118
  12.3 0.4 collective-permute-start
  12.7 37.6 %collective-permute-done = f32[6,128]{1,0:T(8,128)S(1)} collective-permute-done((f32[6,128]{1,0:T(8,128)S(1)}, f32[6,128]{1,0:T(8,128)S(1)}, u32[]{:S(2)}, u32[]{:S(2)}) %collective-permute-start) | collective-permute-done | bytes 3104 | tf_op jit(solution)/shard_map/ppermute | solution.py:118
  50.3 0.0 collective-permute-done.1
  50.3 2.3 %all-to-all-done = bf16[8,32,3584]{2,1,0:T(8,128)(2,1)S(1)} async-done(((bf16[8,32,3584]{2,1,0:T(8,128)(2,1)}), bf16[8,32,3584]{2,1,0:T(8,128)(2,1)S(1)}, u32[]{:S(2)}, u32[]{:S(2)}) %all-to-all-start) | async-done | bytes 1835040 | tf_op jit(solution)/shard_map/all_to_all | solution.py:122
  52.6 0.1 fusion.8
  52.7 0.3 reduce_window_sum.18
  53.0 0.1 fusion.7
  53.1 0.1 fusion.5
  53.2 0.1 fusion.2
  53.3 0.6 convolution_convert_fusion
  54.0 27.5 %all_to_all.20 = bf16[8,32,3584]{2,1,0:T(8,128)(2,1)S(1)} all-to-all(bf16[8,32,3584]{2,1,0:T(8,128)(2,1)S(1)} %bitcast.83), channel_id=1, replica_groups={{0,1,4,5,8,9,12,13},{2,3,6,7,10,11,14,15},{16,17,20,21,24,25,28,29},{18..., dimensions={0} | all-to-all | bytes 3670016 | tf_op jit(solution)/shard_map/all_to_all | solution.py:122
  81.4 9.8 %shard_map.65 = bf16[256,3584]{1,0:T(8,128)(2,1)S(1)} custom-call(bf16[256,3584]{1,0:T(8,128)(2,1)S(1)} %bitcast.73, bf16[3584,1024]{1,0:T(8,128)(2,1)} %bitcast.74, bf16[3584,1024]{1,0:T(8,128)(2,1)} %bitcast.76, bf16[1024,3584]{1,0:T(8,128)(2,1)} %bitcast.78), custom_call_target="tpu_custom_call" | custom-call | flops 5637144576 | bytes 25690112 | tf_op jit(solution)/shard_map/pallas_call | solution.py:82
  91.2 1.2 copy-done.1
  92.5 4.3 %all-to-all-start.3 = ((bf16[8,32,3584]{2,1,0:T(8,128)(2,1)}), bf16[8,32,3584]{2,1,0:T(8,128)(2,1)}, u32[]{:S(2)}, u32[]{:S(2)}) async-start(bf16[8,32,3584]{2,1,0:T(8,128)(2,1)} %bitcast.72), calls=%async_computation.3 | async-start | bytes 3670016 | tf_op jit(solution)/shard_map/all_to_all | solution.py:122
  96.8 9.8 %shard_map.64 = bf16[256,3584]{1,0:T(8,128)(2,1)S(1)} custom-call(bf16[256,3584]{1,0:T(8,128)(2,1)S(1)} %bitcast.70, bf16[3584,1024]{1,0:T(8,128)(2,1)} %bitcast.75, bf16[3584,1024]{1,0:T(8,128)(2,1)} %bitcast.77, bf16[1024,3584]{1,0:T(8,128)(2,1)} %bitcast.79), custom_call_target="tpu_custom_call" | custom-call | flops 5637144576 | bytes 25690112 | tf_op jit(solution)/shard_map/pallas_call | solution.py:82
  106.6 1.2 copy-done
  107.8 12.2 %all-to-all-done.3 = bf16[8,32,3584]{2,1,0:T(8,128)(2,1)} async-done(((bf16[8,32,3584]{2,1,0:T(8,128)(2,1)}), bf16[8,32,3584]{2,1,0:T(8,128)(2,1)}, u32[]{:S(2)}, u32[]{:S(2)}) %all-to-all-start.3) | async-done | bytes 1835040 | tf_op jit(solution)/shard_map/all_to_all | solution.py:122
  120.0 3.6 %all-to-all-start.1 = ((bf16[8,32,3584]{2,1,0:T(8,128)(2,1)}), bf16[8,32,3584]{2,1,0:T(8,128)(2,1)S(1)}, u32[]{:S(2)}, u32[]{:S(2)}) async-start(bf16[8,32,3584]{2,1,0:T(8,128)(2,1)} %bitcast.71), calls=%async_computation.1 | async-start | bytes 3670016 | tf_op jit(solution)/shard_map/all_to_all | solution.py:122
  123.7 1.9 %fusion.15 = f32[128,3584]{1,0:T(8,128)S(1)} fusion(bf16[256,128]{1,0:T(8,128)(2,1)S(1)} %get-tuple-element.19, bf16[256,3584]{1,0:T(8,128)(2,1)} %bitcast.18), kind=kOutput, calls=%fused_computation.42 | convolution fusion | flops 234881024 | bytes 3735552 | tf_op jit(solution)/shard_map/dot_general | solution.py:34
  125.6 2.0 %fusion = bf16[128,3584]{1,0:T(8,128)(2,1)S(1)} fusion(f32[128,3584]{1,0:T(8,128)S(1)} %fusion.15, bf16[256,128]{1,0:T(8,128)(2,1)S(1)} %get-tuple-element.22, bf16[256,3584]{1,0:T(8,128)(2,1)} %bitcast.18), kind=kOutput, calls=%fused_computation.4 | convolution fusion | flops 235798528 | bytes 4653056 | tf_op jit(solution)/shard_map/dot_general | solution.py:35
  127.5 2.8 %collective-permute-start.2 = (bf16[128,3584]{1,0:T(8,128)(2,1)S(1)}, bf16[128,3584]{1,0:T(8,128)(2,1)}, u32[]{:S(2)}, u32[]{:S(2)}) collective-permute-start(bf16[128,3584]{1,0:T(8,128)(2,1)S(1)} %fusion), channel_id=1, source_target_pairs={{0,2},{1,3},{2,0},{3,1},{4,6},{5,7},{6,4},{7,5},{8,10},{9,11},{10,... | collective-permute-start | bytes 2752520 | tf_op jit(solution)/shard_map/ppermute | solution.py:118
  130.3 33.3 %all-to-all-done.1 = bf16[8,32,3584]{2,1,0:T(8,128)(2,1)S(1)} async-done(((bf16[8,32,3584]{2,1,0:T(8,128)(2,1)}), bf16[8,32,3584]{2,1,0:T(8,128)(2,1)S(1)}, u32[]{:S(2)}, u32[]{:S(2)}) %all-to-all-start.1) | async-done | bytes 1835040 | tf_op jit(solution)/shard_map/all_to_all | solution.py:122
  163.7 0.4 fusion.14
  164.1 7.0 %collective-permute-done.2 = bf16[128,3584]{1,0:T(8,128)(2,1)} collective-permute-done((bf16[128,3584]{1,0:T(8,128)(2,1)S(1)}, bf16[128,3584]{1,0:T(8,128)(2,1)}, u32[]{:S(2)}, u32[]{:S(2)}) %collective-permute-start.2) | collective-permute-done | bytes 917536 | tf_op jit(solution)/shard_map/ppermute | solution.py:118
  171.1 2.6 %add_convert_fusion = bf16[128,3584]{1,0:T(8,128)(2,1)} fusion(bf16[128,3584]{1,0:T(8,128)(2,1)} %collective-permute-done.2, f32[128,3584]{1,0:T(8,128)S(1)} %fusion.14, bf16[256,128]{1,0:T(8,128)(2,1)S(1)} %get-tuple-element.18, bf16[256,3584]{1,0:T(8,128)(2,1)S(1)} %bitcast.81), kind=kOutput, calls=%fused_computation.5 | convolution fusion | flops 236716032 | bytes 5570560 | tf_op jit(solution)/shard_map/dot_general | solution.py:35
  (15 shorter events, 0.1 us)
Async XLA Ops:
  4.3 8.0 %copy-start.2 = (s32[128,3]{0,1:T(4,128)S(1)}, s32[128,3]{0,1:T(4,128)}, u32[]{:S(2)}) copy-start(s32[128,3]{0,1:T(4,128)} %param.7) | copy-start | bytes 4612
  4.3 8.0 %copy-start.3 = (f32[128,3]{0,1:T(4,128)S(1)}, f32[128,3]{0,1:T(4,128)}, u32[]{:S(2)}) copy-start(f32[128,3]{0,1:T(4,128)} %param.8) | copy-start | bytes 4612
  4.3 48.3 %all-to-all-start = ((bf16[8,32,3584]{2,1,0:T(8,128)(2,1)}), bf16[8,32,3584]{2,1,0:T(8,128)(2,1)S(1)}, u32[]{:S(2)}, u32[]{:S(2)}) async-start(bf16[8,32,3584]{2,1,0:T(8,128)(2,1)} %bitcast.82), calls=%async_computation | async-start | bytes 3670016 | tf_op jit(solution)/shard_map/all_to_all | solution.py:122
  9.7 40.6 %collective-permute-start.1 = (bf16[128,3584]{1,0:T(8,128)(2,1)}, bf16[128,3584]{1,0:T(8,128)(2,1)S(1)}, u32[]{:S(2)}, u32[]{:S(2)}) collective-permute-start(bf16[128,3584]{1,0:T(8,128)(2,1)} %param.6), channel_id=1, source_target_pairs={{0,2},{1,3},{2,0},{3,1},{4,6},{5,7},{6,4},{7,5},{8,10},{9,11},{10,... | collective-permute-start | bytes 2752520 | tf_op jit(solution)/shard_map/ppermute | solution.py:118
  12.3 38.0 %collective-permute-start = (f32[6,128]{1,0:T(8,128)S(1)}, f32[6,128]{1,0:T(8,128)S(1)}, u32[]{:S(2)}, u32[]{:S(2)}) collective-permute-start(f32[6,128]{1,0:T(8,128)S(1)} %pad_maximum_fusion), channel_id=1, source_target_pairs={{0,2},{1,3},{2,0},{3,1},{4,6},{5,7},{6,4},{7,5},{8,10},{9,11},{10,... | collective-permute-start | bytes 9224 | tf_op jit(solution)/shard_map/ppermute | solution.py:118
  91.2 1.3 copy-start.1
  92.5 27.6 %all-to-all-start.3 = ((bf16[8,32,3584]{2,1,0:T(8,128)(2,1)}), bf16[8,32,3584]{2,1,0:T(8,128)(2,1)}, u32[]{:S(2)}, u32[]{:S(2)}) async-start(bf16[8,32,3584]{2,1,0:T(8,128)(2,1)} %bitcast.72), calls=%async_computation.3 | async-start | bytes 3670016 | tf_op jit(solution)/shard_map/all_to_all | solution.py:122
  106.6 1.3 copy-start
  120.0 43.6 %all-to-all-start.1 = ((bf16[8,32,3584]{2,1,0:T(8,128)(2,1)}), bf16[8,32,3584]{2,1,0:T(8,128)(2,1)S(1)}, u32[]{:S(2)}, u32[]{:S(2)}) async-start(bf16[8,32,3584]{2,1,0:T(8,128)(2,1)} %bitcast.71), calls=%async_computation.1 | async-start | bytes 3670016 | tf_op jit(solution)/shard_map/all_to_all | solution.py:122
  127.5 43.5 %collective-permute-start.2 = (bf16[128,3584]{1,0:T(8,128)(2,1)S(1)}, bf16[128,3584]{1,0:T(8,128)(2,1)}, u32[]{:S(2)}, u32[]{:S(2)}) collective-permute-start(bf16[128,3584]{1,0:T(8,128)(2,1)S(1)} %fusion), channel_id=1, source_target_pairs={{0,2},{1,3},{2,0},{3,1},{4,6},{5,7},{6,4},{7,5},{8,10},{9,11},{10,... | collective-permute-start | bytes 2752520 | tf_op jit(solution)/shard_map/ppermute | solution.py:118

commit v3 on v2

--- a/solution.py
+++ b/solution.py
@@ -37,7 +37,7 @@
 
 VMEM_WHOLE = pl.BlockSpec(memory_space=pltpu.VMEM)
 HBM_WHOLE = pl.BlockSpec(memory_space=pl.ANY)
-UP_GROUPS, DOWN_GROUPS, LANES = 4, 2, 512
+UP_GROUPS, DOWN_GROUPS, LANES = 7, 2, 512
 
 
 def groups_of(size, count):
@@ -130,8 +130,9 @@
     shards = member // half * local_count + first + member % half
 
     pick, high, low = routing(ids, weights, shards, wsplit, capacity)
-    rows = swap(dot(pick, tokens).astype(jnp.bfloat16))
-    rows, table, far_tokens = lax.optimization_barrier((rows, table, far_tokens))
+    packed = dot(pick, tokens).astype(jnp.bfloat16)
+    rows = swap(packed)
+    far_tokens, table, _ = lax.optimization_barrier((far_tokens, table, packed))
     far_pick, far_high, far_low = routing(
         table[:top_count].astype(jnp.int32), table[top_count:], shards, wsplit, capacity
     )

time: 174 us -> 181 us (1.040)
  waiting for transfers between devices: 92.5 us -> 98.5 us
    all_to_all x3, waiting for transfers between devices: 47.9 us -> 56.5 us  [swap(): lax.all_to_all(rows.reshape(members, capacity, width), AXES, 0, 0, axis_i...]
    ppermute x3, waiting for transfers between devices: 44.6 us -> 42 us  [cross(): return lax.ppermute(array, 'local', across)]
  transfers between devices with their start and end apart: 6 -> 6, of which waited for: 5 -> 5; matrix products, arithmetic and copies ran while one was open for 2% -> 6% of each run, Pallas kernels for 6% -> 11%
where the time goes in v3:
time: 181 us; the launch traced here: 180 us
  waiting for transfers between devices  98.5 us (54%)
  blocking collectives  26.3 us (15%)
  Pallas kernels  20.1 us (11%)
  starting transfers between devices  18.8 us (10%)
  matrix products  10.6 us (6%)
  other arithmetic  3.23 us (2%)
  local copies, waits for them, and re-layouts  2.83 us (2%)
    all_to_all x3, waiting for transfers between devices, swap(): lax.all_to_all(rows.reshape(members, capacity, width), AXES, 0, 0, axis_i...  56.5 us
    ppermute x3, waiting for transfers between devices, cross(): return lax.ppermute(array, 'local', across)  42 us
    all_to_all x1, blocking collectives, swap(): lax.all_to_all(rows.reshape(members, capacity, width), AXES, 0, 0, axis_i...  26.3 us
    pallas_call x2, Pallas kernels, ffn(): pl.pallas_call(ffn_kernel, in_specs=[VMEM_WHOLE] + [HBM_WHOLE] * 3, out_s...  20.1 us
    all_to_all x3, starting transfers between devices, swap(): lax.all_to_all(rows.reshape(members, capacity, width), AXES, 0, 0, axis_i...  11.5 us
    ppermute x3, starting transfers between devices, cross(): return lax.ppermute(array, 'local', across)  7.25 us
    dot_general x2, matrix products, weighted_rows(): lax.dot_general(low, rows, contract, preferred_element_type=jnp.float32)  4.59 us
    dot_general x2, matrix products, dot(): return jnp.dot(a, b, preferred_element_type=jnp.float32)  3.66 us
  transfers between devices with their start and end apart: 6, of which 5 were waited for; matrix products, arithmetic and copies ran while one was open for 6% of the time, Pallas kernels for 11%

profile of v3, /device:TPU:0, one launch (start us, length us, event | category | flops | bytes accessed | tf_op | source)
XLA Modules:
  0.0 180.5 jit_solution(14351206756478273875)
XLA Ops:
  0.0 4.1 %collective-permute-start = (bf16[128,3584]{1,0:T(8,128)(2,1)}, bf16[128,3584]{1,0:T(8,128)(2,1)S(1)}, u32[]{:S(2)}, u32[]{:S(2)}) collective-permute-start(bf16[128,3584]{1,0:T(8,128)(2,1)} %param.6), channel_id=1, source_target_pairs={{0,2},{1,3},{2,0},{3,1},{4,6},{5,7},{6,4},{7,5},{8,10},{9,11},{10,... | collective-permute-start | bytes 2752520 | tf_op jit(solution)/shard_map/ppermute | solution.py:118
  4.1 0.7 bitcast_convert_fusion
  4.8 0.7 pad_maximum_fusion
  5.5 0.8 fusion.6
  6.3 0.3 reduce_window_sum.17
  6.6 0.1 eq.93
  6.7 0.1 fusion.3
  6.8 3.0 %convolution_convert_fusion.1 = bf16[256,3584]{1,0:T(8,128)(2,1)} fusion(pred[256,128]{1,0:T(32,128)(4,1)S(1)} %fusion.3, bf16[128,3584]{1,0:T(8,128)(2,1)} %param.6), kind=kOutput, calls=%fused_computation.1 | convolution fusion | flops 235798528 | bytes 2785280 | tf_op jit(solution)/shard_map/dot_general | solution.py:14
  9.8 34.7 %collective-permute-done.1 = f32[6,128]{1,0:T(8,128)S(1)} collective-permute-done((f32[6,128]{1,0:T(8,128)S(1)}, f32[6,128]{1,0:T(8,128)S(1)}, u32[]{:S(2)}, u32[]{:S(2)}) %collective-permute-start.1) | collective-permute-done | bytes 3104 | tf_op jit(solution)/shard_map/ppermute | solution.py:118
  44.5 0.1 fusion.8
  44.5 0.3 reduce_window_sum.18
  44.8 0.1 fusion.7
  44.9 0.1 fusion.5
  45.0 0.1 fusion.2
  45.2 0.6 convolution_convert_fusion
  45.8 26.3 %all_to_all.20 = bf16[8,32,3584]{2,1,0:T(8,128)(2,1)} all-to-all(bf16[8,32,3584]{2,1,0:T(8,128)(2,1)S(1)} %bitcast.82), channel_id=1, replica_groups={{0,1,4,5,8,9,12,13},{2,3,6,7,10,11,14,15},{16,17,20,21,24,25,28,29},{18..., dimensions={0} | all-to-all | bytes 3670016 | tf_op jit(solution)/shard_map/all_to_all | solution.py:122
  72.1 3.6 %all-to-all-start = ((bf16[8,32,3584]{2,1,0:T(8,128)(2,1)}), bf16[8,32,3584]{2,1,0:T(8,128)(2,1)S(1)}, u32[]{:S(2)}, u32[]{:S(2)}) async-start(bf16[8,32,3584]{2,1,0:T(8,128)(2,1)} %bitcast.81), calls=%async_computation | async-start | bytes 3670016 | tf_op jit(solution)/shard_map/all_to_all | solution.py:122
  75.8 1.5 copy-done.1
  77.2 9.5 %shard_map.65 = bf16[256,3584]{1,0:T(8,128)(2,1)S(1)} custom-call(bf16[256,3584]{1,0:T(8,128)(2,1)S(1)} %bitcast.72, bf16[3584,1024]{1,0:T(8,128)(2,1)} %bitcast.73, bf16[3584,1024]{1,0:T(8,128)(2,1)} %bitcast.75, bf16[1024,3584]{1,0:T(8,128)(2,1)} %bitcast.77), custom_call_target="tpu_custom_call" | custom-call | flops 5637144576 | bytes 25690112 | tf_op jit(solution)/shard_map/pallas_call | solution.py:82
  86.7 1.2 copy-done
  88.0 11.0 %all-to-all-done = bf16[8,32,3584]{2,1,0:T(8,128)(2,1)S(1)} async-done(((bf16[8,32,3584]{2,1,0:T(8,128)(2,1)}), bf16[8,32,3584]{2,1,0:T(8,128)(2,1)S(1)}, u32[]{:S(2)}, u32[]{:S(2)}) %all-to-all-start) | async-done | bytes 1835040 | tf_op jit(solution)/shard_map/all_to_all | solution.py:122
  98.9 4.3 %all-to-all-start.3 = ((bf16[8,32,3584]{2,1,0:T(8,128)(2,1)}), bf16[8,32,3584]{2,1,0:T(8,128)(2,1)}, u32[]{:S(2)}, u32[]{:S(2)}) async-start(bf16[8,32,3584]{2,1,0:T(8,128)(2,1)} %bitcast.71), calls=%async_computation.3 | async-start | bytes 3670016 | tf_op jit(solution)/shard_map/all_to_all | solution.py:122
  103.2 10.7 %shard_map.64 = bf16[256,3584]{1,0:T(8,128)(2,1)} custom-call(bf16[256,3584]{1,0:T(8,128)(2,1)S(1)} %bitcast.70, bf16[3584,1024]{1,0:T(8,128)(2,1)} %bitcast.74, bf16[3584,1024]{1,0:T(8,128)(2,1)} %bitcast.76, bf16[1024,3584]{1,0:T(8,128)(2,1)} %bitcast.78), custom_call_target="tpu_custom_call" | custom-call | flops 5637144576 | bytes 25690112 | tf_op jit(solution)/shard_map/pallas_call | solution.py:82
  113.9 12.6 %all-to-all-done.3 = bf16[8,32,3584]{2,1,0:T(8,128)(2,1)} async-done(((bf16[8,32,3584]{2,1,0:T(8,128)(2,1)}), bf16[8,32,3584]{2,1,0:T(8,128)(2,1)}, u32[]{:S(2)}, u32[]{:S(2)}) %all-to-all-start.3) | async-done | bytes 1835040 | tf_op jit(solution)/shard_map/all_to_all | solution.py:122
  126.5 3.6 %all-to-all-start.1 = ((bf16[8,32,3584]{2,1,0:T(8,128)(2,1)}), bf16[8,32,3584]{2,1,0:T(8,128)(2,1)S(1)}, u32[]{:S(2)}, u32[]{:S(2)}) async-start(bf16[8,32,3584]{2,1,0:T(8,128)(2,1)} %bitcast.13), calls=%async_computation.1 | async-start | bytes 3670016 | tf_op jit(solution)/shard_map/all_to_all | solution.py:122
  130.1 1.9 %fusion.15 = f32[128,3584]{1,0:T(8,128)S(1)} fusion(bf16[256,128]{1,0:T(8,128)(2,1)S(1)} %get-tuple-element.17, bf16[256,3584]{1,0:T(8,128)(2,1)} %bitcast.18), kind=kOutput, calls=%fused_computation.42 | convolution fusion | flops 234881024 | bytes 3735552 | tf_op jit(solution)/shard_map/dot_general | solution.py:34
  132.0 2.0 %fusion = bf16[128,3584]{1,0:T(8,128)(2,1)S(1)} fusion(f32[128,3584]{1,0:T(8,128)S(1)} %fusion.15, bf16[256,128]{1,0:T(8,128)(2,1)S(1)} %get-tuple-element.20, bf16[256,3584]{1,0:T(8,128)(2,1)} %bitcast.18), kind=kOutput, calls=%fused_computation.4 | convolution fusion | flops 235798528 | bytes 4653056 | tf_op jit(solution)/shard_map/dot_general | solution.py:35
  134.0 3.1 %collective-permute-start.2 = (bf16[128,3584]{1,0:T(8,128)(2,1)S(1)}, bf16[128,3584]{1,0:T(8,128)(2,1)}, u32[]{:S(2)}, u32[]{:S(2)}) collective-permute-start(bf16[128,3584]{1,0:T(8,128)(2,1)S(1)} %fusion), channel_id=1, source_target_pairs={{0,2},{1,3},{2,0},{3,1},{4,6},{5,7},{6,4},{7,5},{8,10},{9,11},{10,... | collective-permute-start | bytes 2752520 | tf_op jit(solution)/shard_map/ppermute | solution.py:118
  137.1 33.0 %all-to-all-done.1 = bf16[8,32,3584]{2,1,0:T(8,128)(2,1)S(1)} async-done(((bf16[8,32,3584]{2,1,0:T(8,128)(2,1)}), bf16[8,32,3584]{2,1,0:T(8,128)(2,1)S(1)}, u32[]{:S(2)}, u32[]{:S(2)}) %all-to-all-start.1) | async-done | bytes 1835040 | tf_op jit(solution)/shard_map/all_to_all | solution.py:122
  170.1 0.4 fusion.14
  170.5 7.3 %collective-permute-done.2 = bf16[128,3584]{1,0:T(8,128)(2,1)} collective-permute-done((bf16[128,3584]{1,0:T(8,128)(2,1)S(1)}, bf16[128,3584]{1,0:T(8,128)(2,1)}, u32[]{:S(2)}, u32[]{:S(2)}) %collective-permute-start.2) | collective-permute-done | bytes 917536 | tf_op jit(solution)/shard_map/ppermute | solution.py:118
  177.9 2.6 %add_convert_fusion = bf16[128,3584]{1,0:T(8,128)(2,1)} fusion(bf16[128,3584]{1,0:T(8,128)(2,1)} %collective-permute-done.2, f32[128,3584]{1,0:T(8,128)S(1)} %fusion.14, bf16[256,128]{1,0:T(8,128)(2,1)S(1)} %get-tuple-element.16, bf16[256,3584]{1,0:T(8,128)(2,1)S(1)} %bitcast.80), kind=kOutput, calls=%fused_computation.5 | convolution fusion | flops 236716032 | bytes 5570560 | tf_op jit(solution)/shard_map/dot_general | solution.py:35
  (15 shorter events, 0.1 us)
Async XLA Ops:
  0.0 44.8 %copy-start.2 = (s32[128,3]{0,1:T(4,128)S(1)}, s32[128,3]{0,1:T(4,128)}, u32[]{:S(2)}) copy-start(s32[128,3]{0,1:T(4,128)} %param.7) | copy-start | bytes 4612
  0.0 44.8 %copy-start.3 = (f32[128,3]{0,1:T(4,128)S(1)}, f32[128,3]{0,1:T(4,128)}, u32[]{:S(2)}) copy-start(f32[128,3]{0,1:T(4,128)} %param.8) | copy-start | bytes 4612
  0.0 44.5 %collective-permute-start = (bf16[128,3584]{1,0:T(8,128)(2,1)}, bf16[128,3584]{1,0:T(8,128)(2,1)S(1)}, u32[]{:S(2)}, u32[]{:S(2)}) collective-permute-start(bf16[128,3584]{1,0:T(8,128)(2,1)} %param.6), channel_id=1, source_target_pairs={{0,2},{1,3},{2,0},{3,1},{4,6},{5,7},{6,4},{7,5},{8,10},{9,11},{10,... | collective-permute-start | bytes 2752520 | tf_op jit(solution)/shard_map/ppermute | solution.py:118
  5.4 39.0 %collective-permute-start.1 = (f32[6,128]{1,0:T(8,128)S(1)}, f32[6,128]{1,0:T(8,128)S(1)}, u32[]{:S(2)}, u32[]{:S(2)}) collective-permute-start(f32[6,128]{1,0:T(8,128)S(1)} %pad_maximum_fusion), channel_id=1, source_target_pairs={{0,2},{1,3},{2,0},{3,1},{4,6},{5,7},{6,4},{7,5},{8,10},{9,11},{10,... | collective-permute-start | bytes 9224 | tf_op jit(solution)/shard_map/ppermute | solution.py:118
  72.1 26.8 %all-to-all-start = ((bf16[8,32,3584]{2,1,0:T(8,128)(2,1)}), bf16[8,32,3584]{2,1,0:T(8,128)(2,1)S(1)}, u32[]{:S(2)}, u32[]{:S(2)}) async-start(bf16[8,32,3584]{2,1,0:T(8,128)(2,1)} %bitcast.81), calls=%async_computation | async-start | bytes 3670016 | tf_op jit(solution)/shard_map/all_to_all | solution.py:122
  75.7 1.5 copy-start.1
  86.7 1.3 copy-start
  98.9 27.6 %all-to-all-start.3 = ((bf16[8,32,3584]{2,1,0:T(8,128)(2,1)}), bf16[8,32,3584]{2,1,0:T(8,128)(2,1)}, u32[]{:S(2)}, u32[]{:S(2)}) async-start(bf16[8,32,3584]{2,1,0:T(8,128)(2,1)} %bitcast.71), calls=%async_computation.3 | async-start | bytes 3670016 | tf_op jit(solution)/shard_map/all_to_all | solution.py:122
  126.5 43.6 %all-to-all-start.1 = ((bf16[8,32,3584]{2,1,0:T(8,128)(2,1)}), bf16[8,32,3584]{2,1,0:T(8,128)(2,1)S(1)}, u32[]{:S(2)}, u32[]{:S(2)}) async-start(bf16[8,32,3584]{2,1,0:T(8,128)(2,1)} %bitcast.13), calls=%async_computation.1 | async-start | bytes 3670016 | tf_op jit(solution)/shard_map/all_to_all | solution.py:122
  134.0 43.9 %collective-permute-start.2 = (bf16[128,3584]{1,0:T(8,128)(2,1)S(1)}, bf16[128,3584]{1,0:T(8,128)(2,1)}, u32[]{:S(2)}, u32[]{:S(2)}) collective-permute-start(bf16[128,3584]{1,0:T(8,128)(2,1)S(1)} %fusion), channel_id=1, source_target_pairs={{0,2},{1,3},{2,0},{3,1},{4,6},{5,7},{6,4},{7,5},{8,10},{9,11},{10,... | collective-permute-start | bytes 2752520 | tf_op jit(solution)/shard_map/ppermute | solution.py:118

commit v4 on v3

--- a/solution.py
+++ b/solution.py
@@ -37,7 +37,7 @@
 
 VMEM_WHOLE = pl.BlockSpec(memory_space=pltpu.VMEM)
 HBM_WHOLE = pl.BlockSpec(memory_space=pl.ANY)
-UP_GROUPS, DOWN_GROUPS, LANES = 7, 2, 512
+UP_GROUPS, DOWN_GROUPS, LANES = 7, 1, 512
 
 
 def groups_of(size, count):
@@ -123,7 +123,7 @@
         return moved.reshape(slots, width)
 
     ids, weights = expert_ids.T, gate_weights.T
-    table = cross(jnp.concatenate([ids.astype(jnp.float32), weights]))
+    table = cross(jnp.concatenate([expert_ids.astype(jnp.float32), gate_weights], axis=1))
     far_tokens = cross(tokens)
     member = jnp.arange(members, dtype=jnp.int32)
     first = lax.axis_index("local") // half * half
@@ -134,7 +134,7 @@
     rows = swap(packed)
     far_tokens, table, _ = lax.optimization_barrier((far_tokens, table, packed))
     far_pick, far_high, far_low = routing(
-        table[:top_count].astype(jnp.int32), table[top_count:], shards, wsplit, capacity
+        table[:, :top_count].T.astype(jnp.int32), table[:, top_count:].T, shards, wsplit, capacity
     )
     far_tokens, far_pick, far_high, far_low, high, low = lax.optimization_barrier(
         (far_tokens, far_pick, far_high, far_low, high, low)

time: 181 us -> 181 us (level)
  no operation moved by 1% of the time
where the time goes in v4:
time: 181 us; the launch traced here: 180 us
  waiting for transfers between devices  98.2 us (54%)
  blocking collectives  26.3 us (15%)
  Pallas kernels  20.4 us (11%)
  starting transfers between devices  18.8 us (10%)
  matrix products  10.6 us (6%)
  other arithmetic  3.22 us (2%)
  local copies, waits for them, and re-layouts  2.83 us (2%)
    all_to_all x3, waiting for transfers between devices, swap(): lax.all_to_all(rows.reshape(members, capacity, width), AXES, 0, 0, axis_i...  56.3 us
    ppermute x3, waiting for transfers between devices, cross(): return lax.ppermute(array, 'local', across)  42 us
    all_to_all x1, blocking collectives, swap(): lax.all_to_all(rows.reshape(members, capacity, width), AXES, 0, 0, axis_i...  26.3 us
    pallas_call x2, Pallas kernels, ffn(): pl.pallas_call(ffn_kernel, in_specs=[VMEM_WHOLE] + [HBM_WHOLE] * 3, out_s...  20.4 us
    all_to_all x3, starting transfers between devices, swap(): lax.all_to_all(rows.reshape(members, capacity, width), AXES, 0, 0, axis_i...  11.5 us
    ppermute x3, starting transfers between devices, cross(): return lax.ppermute(array, 'local', across)  7.28 us
    dot_general x2, matrix products, weighted_rows(): lax.dot_general(low, rows, contract, preferred_element_type=jnp.float32)  4.59 us
    dot_general x2, matrix products, dot(): return jnp.dot(a, b, preferred_element_type=jnp.float32)  3.65 us
  transfers between devices with their start and end apart: 6, of which 5 were waited for; matrix products, arithmetic and copies ran while one was open for 6% of the time, Pallas kernels for 11%

profile of v4, /device:TPU:0, one launch (start us, length us, event | category | flops | bytes accessed | tf_op | source)
XLA Modules:
  0.0 180.5 jit_solution(11506449090803845995)
XLA Ops:
  0.0 4.1 %collective-permute-start = (bf16[128,3584]{1,0:T(8,128)(2,1)}, bf16[128,3584]{1,0:T(8,128)(2,1)S(1)}, u32[]{:S(2)}, u32[]{:S(2)}) collective-permute-start(bf16[128,3584]{1,0:T(8,128)(2,1)} %param.6), channel_id=1, source_target_pairs={{0,2},{1,3},{2,0},{3,1},{4,6},{5,7},{6,4},{7,5},{8,10},{9,11},{10,... | collective-permute-start | bytes 2752520 | tf_op jit(solution)/shard_map/ppermute | solution.py:118
  4.1 0.7 convert_element_type.51
  4.8 0.7 pad_maximum_fusion
  5.5 0.8 fusion.6
  6.3 0.3 reduce_window_sum.17
  6.6 0.1 eq.93
  6.7 0.1 fusion.3
  6.8 3.0 %convolution_convert_fusion.1 = bf16[256,3584]{1,0:T(8,128)(2,1)} fusion(pred[256,128]{1,0:T(32,128)(4,1)S(1)} %fusion.3, bf16[128,3584]{1,0:T(8,128)(2,1)} %param.6), kind=kOutput, calls=%fused_computation.1 | convolution fusion | flops 235798528 | bytes 2785280 | tf_op jit(solution)/shard_map/dot_general | solution.py:14
  9.8 34.7 %collective-permute-done.1 = f32[128,6]{0,1:T(8,128)S(1)} collective-permute-done((f32[128,6]{0,1:T(8,128)S(1)}, f32[128,6]{0,1:T(8,128)S(1)}, u32[]{:S(2)}, u32[]{:S(2)}) %collective-permute-start.1) | collective-permute-done | bytes 3104 | tf_op jit(solution)/shard_map/ppermute | solution.py:118
  44.5 0.1 fusion.8
  44.5 0.3 reduce_window_sum.18
  44.9 0.1 fusion.7
  44.9 0.1 fusion.5
  45.0 0.1 fusion.2
  45.2 0.6 convolution_convert_fusion
  45.8 26.3 %all_to_all.20 = bf16[8,32,3584]{2,1,0:T(8,128)(2,1)} all-to-all(bf16[8,32,3584]{2,1,0:T(8,128)(2,1)S(1)} %bitcast.85), channel_id=1, replica_groups={{0,1,4,5,8,9,12,13},{2,3,6,7,10,11,14,15},{16,17,20,21,24,25,28,29},{18..., dimensions={0} | all-to-all | bytes 3670016 | tf_op jit(solution)/shard_map/all_to_all | solution.py:122
  72.1 3.6 %all-to-all-start = ((bf16[8,32,3584]{2,1,0:T(8,128)(2,1)}), bf16[8,32,3584]{2,1,0:T(8,128)(2,1)S(1)}, u32[]{:S(2)}, u32[]{:S(2)}) async-start(bf16[8,32,3584]{2,1,0:T(8,128)(2,1)} %bitcast.84), calls=%async_computation | async-start | bytes 3670016 | tf_op jit(solution)/shard_map/all_to_all | solution.py:122
  75.8 1.5 copy-done.1
  77.2 9.6 %shard_map.65 = bf16[256,3584]{1,0:T(8,128)(2,1)S(1)} custom-call(bf16[256,3584]{1,0:T(8,128)(2,1)S(1)} %bitcast.75, bf16[3584,1024]{1,0:T(8,128)(2,1)} %bitcast.76, bf16[3584,1024]{1,0:T(8,128)(2,1)} %bitcast.78, bf16[1024,3584]{1,0:T(8,128)(2,1)} %bitcast.80), custom_call_target="tpu_custom_call" | custom-call | flops 5637144576 | bytes 25690112 | tf_op jit(solution)/shard_map/pallas_call | solution.py:82
  86.8 1.2 copy-done
  88.1 10.8 %all-to-all-done = bf16[8,32,3584]{2,1,0:T(8,128)(2,1)S(1)} async-done(((bf16[8,32,3584]{2,1,0:T(8,128)(2,1)}), bf16[8,32,3584]{2,1,0:T(8,128)(2,1)S(1)}, u32[]{:S(2)}, u32[]{:S(2)}) %all-to-all-start) | async-done | bytes 1835040 | tf_op jit(solution)/shard_map/all_to_all | solution.py:122
  98.9 4.3 %all-to-all-start.3 = ((bf16[8,32,3584]{2,1,0:T(8,128)(2,1)}), bf16[8,32,3584]{2,1,0:T(8,128)(2,1)}, u32[]{:S(2)}, u32[]{:S(2)}) async-start(bf16[8,32,3584]{2,1,0:T(8,128)(2,1)} %bitcast.74), calls=%async_computation.3 | async-start | bytes 3670016 | tf_op jit(solution)/shard_map/all_to_all | solution.py:122
  103.2 10.8 %shard_map.64 = bf16[256,3584]{1,0:T(8,128)(2,1)} custom-call(bf16[256,3584]{1,0:T(8,128)(2,1)S(1)} %bitcast.73, bf16[3584,1024]{1,0:T(8,128)(2,1)} %bitcast.77, bf16[3584,1024]{1,0:T(8,128)(2,1)} %bitcast.79, bf16[1024,3584]{1,0:T(8,128)(2,1)} %bitcast.81), custom_call_target="tpu_custom_call" | custom-call | flops 5637144576 | bytes 25690112 | tf_op jit(solution)/shard_map/pallas_call | solution.py:82
  114.0 12.4 %all-to-all-done.3 = bf16[8,32,3584]{2,1,0:T(8,128)(2,1)} async-done(((bf16[8,32,3584]{2,1,0:T(8,128)(2,1)}), bf16[8,32,3584]{2,1,0:T(8,128)(2,1)}, u32[]{:S(2)}, u32[]{:S(2)}) %all-to-all-start.3) | async-done | bytes 1835040 | tf_op jit(solution)/shard_map/all_to_all | solution.py:122
  126.5 3.6 %all-to-all-start.1 = ((bf16[8,32,3584]{2,1,0:T(8,128)(2,1)}), bf16[8,32,3584]{2,1,0:T(8,128)(2,1)S(1)}, u32[]{:S(2)}, u32[]{:S(2)}) async-start(bf16[8,32,3584]{2,1,0:T(8,128)(2,1)} %bitcast.15), calls=%async_computation.1 | async-start | bytes 3670016 | tf_op jit(solution)/shard_map/all_to_all | solution.py:122
  130.1 1.9 %fusion.14 = f32[128,3584]{1,0:T(8,128)S(1)} fusion(bf16[256,128]{1,0:T(8,128)(2,1)S(1)} %get-tuple-element.17, bf16[256,3584]{1,0:T(8,128)(2,1)} %bitcast.20), kind=kOutput, calls=%fused_computation.41 | convolution fusion | flops 234881024 | bytes 3735552 | tf_op jit(solution)/shard_map/dot_general | solution.py:34
  132.0 2.0 %fusion = bf16[128,3584]{1,0:T(8,128)(2,1)S(1)} fusion(f32[128,3584]{1,0:T(8,128)S(1)} %fusion.14, bf16[256,128]{1,0:T(8,128)(2,1)S(1)} %get-tuple-element.20, bf16[256,3584]{1,0:T(8,128)(2,1)} %bitcast.20), kind=kOutput, calls=%fused_computation.4 | convolution fusion | flops 235798528 | bytes 4653056 | tf_op jit(solution)/shard_map/dot_general | solution.py:35
  134.0 3.1 %collective-permute-start.2 = (bf16[128,3584]{1,0:T(8,128)(2,1)S(1)}, bf16[128,3584]{1,0:T(8,128)(2,1)}, u32[]{:S(2)}, u32[]{:S(2)}) collective-permute-start(bf16[128,3584]{1,0:T(8,128)(2,1)S(1)} %fusion), channel_id=1, source_target_pairs={{0,2},{1,3},{2,0},{3,1},{4,6},{5,7},{6,4},{7,5},{8,10},{9,11},{10,... | collective-permute-start | bytes 2752520 | tf_op jit(solution)/shard_map/ppermute | solution.py:118
  137.1 33.0 %all-to-all-done.1 = bf16[8,32,3584]{2,1,0:T(8,128)(2,1)S(1)} async-done(((bf16[8,32,3584]{2,1,0:T(8,128)(2,1)}), bf16[8,32,3584]{2,1,0:T(8,128)(2,1)S(1)}, u32[]{:S(2)}, u32[]{:S(2)}) %all-to-all-start.1) | async-done | bytes 1835040 | tf_op jit(solution)/shard_map/all_to_all | solution.py:122
  170.1 0.4 fusion.13
  170.6 7.3 %collective-permute-done.2 = bf16[128,3584]{1,0:T(8,128)(2,1)} collective-permute-done((bf16[128,3584]{1,0:T(8,128)(2,1)S(1)}, bf16[128,3584]{1,0:T(8,128)(2,1)}, u32[]{:S(2)}, u32[]{:S(2)}) %collective-permute-start.2) | collective-permute-done | bytes 917536 | tf_op jit(solution)/shard_map/ppermute | solution.py:118
  177.9 2.6 %add_convert_fusion = bf16[128,3584]{1,0:T(8,128)(2,1)} fusion(bf16[128,3584]{1,0:T(8,128)(2,1)} %collective-permute-done.2, f32[128,3584]{1,0:T(8,128)S(1)} %fusion.13, bf16[256,128]{1,0:T(8,128)(2,1)S(1)} %get-tuple-element.16, bf16[256,3584]{1,0:T(8,128)(2,1)S(1)} %bitcast.83), kind=kOutput, calls=%fused_computation.5 | convolution fusion | flops 236716032 | bytes 5570560 | tf_op jit(solution)/shard_map/dot_general | solution.py:35
  (15 shorter events, 0.1 us)
Async XLA Ops:
  0.0 44.8 %copy-start.2 = (s32[128,3]{0,1:T(4,128)S(1)}, s32[128,3]{0,1:T(4,128)}, u32[]{:S(2)}) copy-start(s32[128,3]{0,1:T(4,128)} %param.7) | copy-start | bytes 4612
  0.0 44.8 %copy-start.3 = (f32[128,3]{0,1:T(4,128)S(1)}, f32[128,3]{0,1:T(4,128)}, u32[]{:S(2)}) copy-start(f32[128,3]{0,1:T(4,128)} %param.8) | copy-start | bytes 4612
  0.0 44.5 %collective-permute-start = (bf16[128,3584]{1,0:T(8,128)(2,1)}, bf16[128,3584]{1,0:T(8,128)(2,1)S(1)}, u32[]{:S(2)}, u32[]{:S(2)}) collective-permute-start(bf16[128,3584]{1,0:T(8,128)(2,1)} %param.6), channel_id=1, source_target_pairs={{0,2},{1,3},{2,0},{3,1},{4,6},{5,7},{6,4},{7,5},{8,10},{9,11},{10,... | collective-permute-start | bytes 2752520 | tf_op jit(solution)/shard_map/ppermute | solution.py:118
  5.4 39.0 %collective-permute-start.1 = (f32[128,6]{0,1:T(8,128)S(1)}, f32[128,6]{0,1:T(8,128)S(1)}, u32[]{:S(2)}, u32[]{:S(2)}) collective-permute-start(f32[128,6]{0,1:T(8,128)S(1)} %pad_maximum_fusion), channel_id=1, source_target_pairs={{0,2},{1,3},{2,0},{3,1},{4,6},{5,7},{6,4},{7,5},{8,10},{9,11},{10,... | collective-permute-start | bytes 9224 | tf_op jit(solution)/shard_map/ppermute | solution.py:118
  72.1 26.8 %all-to-all-start = ((bf16[8,32,3584]{2,1,0:T(8,128)(2,1)}), bf16[8,32,3584]{2,1,0:T(8,128)(2,1)S(1)}, u32[]{:S(2)}, u32[]{:S(2)}) async-start(bf16[8,32,3584]{2,1,0:T(8,128)(2,1)} %bitcast.84), calls=%async_computation | async-start | bytes 3670016 | tf_op jit(solution)/shard_map/all_to_all | solution.py:122
  75.7 1.5 copy-start.1
  86.8 1.3 copy-start
  98.9 27.6 %all-to-all-start.3 = ((bf16[8,32,3584]{2,1,0:T(8,128)(2,1)}), bf16[8,32,3584]{2,1,0:T(8,128)(2,1)}, u32[]{:S(2)}, u32[]{:S(2)}) async-start(bf16[8,32,3584]{2,1,0:T(8,128)(2,1)} %bitcast.74), calls=%async_computation.3 | async-start | bytes 3670016 | tf_op jit(solution)/shard_map/all_to_all | solution.py:122
  126.5 43.6 %all-to-all-start.1 = ((bf16[8,32,3584]{2,1,0:T(8,128)(2,1)}), bf16[8,32,3584]{2,1,0:T(8,128)(2,1)S(1)}, u32[]{:S(2)}, u32[]{:S(2)}) async-start(bf16[8,32,3584]{2,1,0:T(8,128)(2,1)} %bitcast.15), calls=%async_computation.1 | async-start | bytes 3670016 | tf_op jit(solution)/shard_map/all_to_all | solution.py:122
  134.0 43.9 %collective-permute-start.2 = (bf16[128,3584]{1,0:T(8,128)(2,1)S(1)}, bf16[128,3584]{1,0:T(8,128)(2,1)}, u32[]{:S(2)}, u32[]{:S(2)}) collective-permute-start(bf16[128,3584]{1,0:T(8,128)(2,1)S(1)} %fusion), channel_id=1, source_target_pairs={{0,2},{1,3},{2,0},{3,1},{4,6},{5,7},{6,4},{7,5},{8,10},{9,11},{10,... | collective-permute-start | bytes 2752520 | tf_op jit(solution)/shard_map/ppermute | solution.py:118
